TPU v7x, 32 devices: a whole 2x2x4 slice. The times are simulated.
32 devices in a mesh: dp: 8 (over z, y), rep: 4 (over x, core).
Axes of the slice: x: 2, y: 2, z: 4, core: 2. Of those that a mesh axis runs over, the one named last changes fastest.
Arguments:
- circuits: bfloat16 [8192, 1024], P(('dp', 'rep')), may hold values from -2.65 to 2.65
- records: bfloat16 [8192, 1024], P(('dp', 'rep')), may hold values from -0.25 to 0.25
- record_gain: float32 [1024], replicated, may hold values from 0.5 to 2
- log_scale: float32 [1], replicated, may hold values from 1.6 to 2.4
- logit_bias: float32 [1], replicated, may hold values from -3 to -1
- hard_ids: int32 [8192, 16], P(('dp', 'rep')), may hold values from -1 to 8191, as said below
Outputs:
- grad_circuits: float32 [8192, 1024], P(('dp', 'rep'))
- grad_records: float32 [8192, 1024], P(('dp', 'rep'))
- grad_gain: float32 [1024], replicated
- statistics: float32 [2], replicated
- mean_loss: float32 [1], replicated
Inputs may be any that keep to these rules, and one draw needn't show every extreme that they name: `hard_ids`: every entry that is not -1 names a row held by a device with the same dp index as the pair's device (the same value of row // 1024). Over the 256 pairs of one device, at most 16 entries name rows of any one device, and in each dp index one device is named exactly 16 times by every device of that dp index.
All inputs are finite; a program needn't handle non-finite values.
Results may differ from a plain program's by a relative error of at most 0.0043.
Values may be sent and summed in bfloat16 or wider, within the bound.
A program may use at most 64 MiB of HBM per device.

v0:
```python
import jax
import jax.numpy as jnp
from jax import lax
from jax.sharding import PartitionSpec as P

HOPS = 4
CAP = 16


EPSILON = 1e-06


def shifted(value, axis, steps):
    count = lax.axis_size(axis)
    pairs = [(source, (source + steps) % count) for source in range(count)]
    return lax.ppermute(value, axis, pairs)


def unit_rows(values):
    sq_total = jnp.sum(values * values, axis=-1, keepdims=True)
    lengths = jnp.sqrt(sq_total + EPSILON)
    return (values / lengths, lengths)


def transposed_product(left, right):
    return lax.dot_general(
        left, right, (((0,), (0,)), ((), ())), preferred_element_type=jnp.float32
    )


def score_tile(circ_block, rec_block, multiplier, bias_value, own_block):
    products = lax.dot_general(
        circ_block, rec_block, (((1,), (1,)), ((), ())), preferred_element_type=jnp.float32
    )
    scores = products * multiplier + bias_value
    weights = jax.nn.sigmoid(scores)
    losses = jax.nn.softplus(scores)
    if own_block:
        tile_rows = scores.shape[0]
        diag_mask = (
            lax.broadcasted_iota(jnp.int32, (tile_rows, tile_rows), 0)
            == lax.broadcasted_iota(jnp.int32, (tile_rows, tile_rows), 1)
        ).astype(jnp.float32)
        weights = weights - diag_mask
        losses = losses - scores * diag_mask
    summary = jnp.stack(
        [jnp.sum(weights * (scores - bias_value)), jnp.sum(weights), jnp.sum(losses)]
    )
    return (weights.astype(jnp.bfloat16), summary)


def per_device(circuits, records, record_gain, log_scale, logit_bias, hard_ids):
    pair_rows = circuits.shape[0]
    list_width = hard_ids.shape[1]
    rep_count = lax.axis_size("rep")
    loop_count = lax.axis_size("dp")
    circ_unit, circ_length = unit_rows(circuits.astype(jnp.float32))
    circ_emb = circ_unit.astype(jnp.bfloat16)
    rec_pre = records.astype(jnp.float32) * record_gain
    rec_unit, rec_length = unit_rows(rec_pre)
    rec_emb = rec_unit.astype(jnp.bfloat16)
    multiplier = jnp.exp(log_scale[0])
    bias_value = logit_bias[0]
    own_weights, summary = score_tile(circ_emb, rec_emb, multiplier, bias_value, True)
    grad_circ = jnp.dot(own_weights, rec_emb, preferred_element_type=jnp.float32)
    running = transposed_product(own_weights, circ_emb)
    visitor = rec_emb
    for hop_index in range(HOPS):
        visitor = shifted(visitor, "dp", -1)
        running = shifted(running, "dp", -1)
        weights, portion = score_tile(circ_emb, visitor, multiplier, bias_value, False)
        grad_circ = grad_circ + jnp.dot(weights, visitor, preferred_element_type=jnp.float32)
        summary = summary + portion
        running = running + transposed_product(weights, circ_emb)
    grad_rec = shifted(running, "dp", HOPS)
    entry_ids = hard_ids.reshape(-1)
    entry_count = entry_ids.shape[0]
    is_live = entry_ids >= 0
    owner_dev = entry_ids // pair_rows % rep_count
    row_within = entry_ids % pair_rows
    owner_hits = (
        (owner_dev[:, None] == jnp.arange(rep_count, dtype=jnp.int32)[None, :]) & is_live[:, None]
    ).astype(jnp.int32)
    before = jnp.cumsum(owner_hits, axis=0) - owner_hits
    slot_index = jnp.sum(before * owner_hits, axis=1)
    slot_total = rep_count * CAP
    target = jnp.where(is_live, owner_dev * CAP + slot_index, slot_total)
    asked_rows = (
        jnp.zeros((slot_total,), jnp.int32)
        .at[target]
        .set(row_within, mode="drop")
        .reshape(rep_count, CAP)
    )
    slot_pair = (
        jnp.zeros((slot_total,), jnp.int32)
        .at[target]
        .set(jnp.arange(entry_count, dtype=jnp.int32) // list_width, mode="drop")
    )
    slot_live = jnp.zeros((slot_total,), jnp.float32).at[target].set(1.0, mode="drop")
    found_rows = jnp.take(
        rec_emb, lax.all_to_all(asked_rows, "rep", split_axis=0, concat_axis=0, tiled=True), axis=0
    )
    fetched = lax.all_to_all(found_rows, "rep", split_axis=0, concat_axis=0, tiled=True)
    fetched = fetched.reshape(slot_total, fetched.shape[2])
    slot_products = lax.dot_general(
        fetched, circ_emb, (((1,), (1,)), ((), ())), preferred_element_type=jnp.float32
    )
    chosen = (slot_pair[:, None] == lax.broadcasted_iota(jnp.int32, (slot_total, pair_rows), 1)) & (
        slot_live[:, None] > 0
    )
    hard_products = jnp.sum(jnp.where(chosen, slot_products, 0.0), axis=1)
    hard_scores = hard_products * multiplier + bias_value
    hard_weights = jnp.where(slot_live > 0, jax.nn.sigmoid(hard_scores), 0.0)
    hard_losses = jnp.where(slot_live > 0, jax.nn.softplus(hard_scores), 0.0)
    spread = jnp.where(
        chosen, hard_weights.astype(jnp.bfloat16)[:, None], jnp.zeros((), jnp.bfloat16)
    )
    hard_grad = transposed_product(spread, fetched)
    summary = summary + jnp.stack(
        [
            jnp.sum(hard_weights * hard_products * multiplier),
            jnp.sum(hard_weights),
            jnp.sum(hard_losses),
        ]
    )
    grad_circ_emb = multiplier * (grad_circ + hard_grad)
    grad_rec_emb = multiplier * grad_rec
    grad_circuits = (
        grad_circ_emb - circ_unit * jnp.sum(circ_unit * grad_circ_emb, axis=-1, keepdims=True)
    ) / circ_length
    grad_pre = (
        grad_rec_emb - rec_unit * jnp.sum(rec_unit * grad_rec_emb, axis=-1, keepdims=True)
    ) / rec_length
    grad_records = grad_pre * record_gain
    gain_part = jnp.sum(records.astype(jnp.float32) * grad_pre, axis=0)
    gain_total, summary_total = lax.psum((gain_part, summary), ("dp", "rep"))
    pair_total = pair_rows * loop_count * rep_count
    statistics = jnp.stack([summary_total[0], summary_total[1]])
    mean_loss = jnp.stack([summary_total[2] / pair_total])
    return (grad_circuits, grad_records, gain_total, statistics, mean_loss)


def solution(mesh):
    placed = (P(("dp", "rep"), None), P(("dp", "rep"), None), P(), P(), P(), P(("dp", "rep"), None))
    return jax.shard_map(
        per_device,
        mesh=mesh,
        in_specs=placed,
        out_specs=(P(("dp", "rep"), None), P(("dp", "rep"), None), P(), P(), P()),
        check_vma=False,
    )
```

profile of v0, /device:TPU:0, one launch (start us, length us, event | category | flops | bytes accessed | tf_op | source)
XLA Modules:
  0.0 261.7 jit_solution(4319335786389604963)
XLA Ops:
  0.6 0.8 copy.14
  1.9 1.2 reduce-window.6
  3.9 15.5 %scatter_custom_fusion.2 = s32[64]{0:T(128)S(1)} fusion(s32[4096]{0:T(1024)S(1)} %bitcast.84, s32[4096]{0:T(1024)S(1)} %get-tuple-element.28, s32[]{:T(128)} %constant.87.clone.1), kind=kCustom, calls=%fused_computation.158 | custom fusion | bytes 260 | tf_op jit(solution)/shard_map/scatter | solution.py:91
  19.4 0.7 all_to_all.13
  20.0 4.2 %all-to-all-start = ((s32[4,1,16]{2,1,0:T(1,128)}), s32[4,1,16]{2,1,0:T(1,128)S(1)}, u32[]{:S(2)}, u32[]{:S(2)}) async-start(s32[4,1,16]{2,1,0:T(1,128)} %bitcast.5), calls=%async_computation | async-start | bytes 4096 | tf_op jit(solution)/shard_map/all_to_all | solution.py:101
  24.7 5.1 %collective-permute-start = (bf16[256,1024]{1,0:T(8,128)(2,1)S(1)}, bf16[256,1024]{1,0:T(8,128)(2,1)}, u32[]{:S(2)}, u32[]{:S(2)}) collective-permute-start(bf16[256,1024]{1,0:T(8,128)(2,1)S(1)} %fusion.77), channel_id=1, source_target_pairs={{0,28},{4,0},{8,4},{12,8},{16,12},{20,16},{24,20},{28,24},{1,29},{... | collective-permute-start | bytes 1572872 | tf_op jit(solution)/shard_map/ppermute | solution.py:16
  31.5 1.2 multiply_reduce_fusion.6
  32.8 1.3 fusion.33
  34.1 0.8 collective-permute-start.4
  34.9 15.5 %scatter_custom_fusion.1 = f32[64]{0:T(128)S(1)} fusion(s32[4096]{0:T(1024)S(1)} %bitcast.85, f32[4096]{0:T(1024)S(1)} %broadcast.271, f32[]{:T(128)} %constant.85.clone.1), kind=kCustom, calls=%fused_computation.156 | custom fusion | bytes 260 | tf_op jit(solution)/shard_map/scatter | solution.py:99
  50.9 0.5 broadcast_compare_fusion.2
  51.4 16.0 %scatter_custom_fusion = s32[64]{0:T(128)} fusion(s32[4096]{0:T(1024)S(1)} %bitcast.86, s32[4096]{0:T(1024)S(1)} %add_select_fusion.1, s32[]{:T(128)} %constant.87.clone.1), kind=kCustom, calls=%fused_computation.160 | custom fusion | bytes 260 | tf_op jit(solution)/shard_map/scatter | solution.py:97
  67.5 1.1 collective-permute-start.1
  68.6 2.3 multiply_reduce_fusion.5
  70.9 2.5 convolution_add_fusion
  73.5 0.8 collective-permute-start.5
  74.3 0.6 pad_clamp_fusion
  74.9 0.8 gather_fusion
  75.7 0.7 broadcast_select_fusion
  76.4 3.3 %all-to-all-start.1 = ((bf16[4,16,1024]{2,1,0:T(8,128)(2,1)}), bf16[4,16,1024]{2,1,0:T(8,128)(2,1)S(1)}, u32[]{:S(2)}, u32[]{:S(2)}) async-start(bf16[4,16,1024]{2,1,0:T(8,128)(2,1)} %broadcast_select_fusion), calls=%async_computation.1 | async-start | bytes 262144 | tf_op jit(solution)/shard_map/all_to_all | solution.py:103
  79.8 2.8 %collective-permute-done.1 = bf16[256,1024]{1,0:T(8,128)(2,1)} collective-permute-done((bf16[256,1024]{1,0:T(8,128)(2,1)}, bf16[256,1024]{1,0:T(8,128)(2,1)}, u32[]{:S(2)}, u32[]{:S(2)}) %collective-permute-start.1) | collective-permute-done | bytes 524320 | tf_op jit(solution)/shard_map/ppermute | solution.py:16
  82.6 2.3 multiply_reduce_fusion.4
  85.2 3.9 %collective-permute-start.2 = (bf16[256,1024]{1,0:T(8,128)(2,1)}, bf16[256,1024]{1,0:T(8,128)(2,1)}, u32[]{:S(2)}, u32[]{:S(2)}) collective-permute-start(bf16[256,1024]{1,0:T(8,128)(2,1)} %collective-permute-done.1), channel_id=1, source_target_pairs={{0,28},{4,0},{8,4},{12,8},{16,12},{20,16},{24,20},{28,24},{1,29},{... | collective-permute-start | bytes 1572872 | tf_op jit(solution)/shard_map/ppermute | solution.py:16
  89.1 16.0 %collective-permute-done.5 = f32[256,1024]{1,0:T(8,128)} collective-permute-done((f32[256,1024]{1,0:T(8,128)}, f32[256,1024]{1,0:T(8,128)}, u32[]{:S(2)}, u32[]{:S(2)}) %collective-permute-start.5) | collective-permute-done | bytes 1048608 | tf_op jit(solution)/shard_map/ppermute | solution.py:16
  105.1 2.3 add.241
  107.4 3.8 %collective-permute-start.6 = (f32[256,1024]{1,0:T(8,128)}, f32[256,1024]{1,0:T(8,128)}, u32[]{:S(2)}, u32[]{:S(2)}) collective-permute-start(f32[256,1024]{1,0:T(8,128)} %add.241), channel_id=1, source_target_pairs={{0,28},{4,0},{8,4},{12,8},{16,12},{20,16},{24,20},{28,24},{1,29},{... | collective-permute-start | bytes 3145736 | tf_op jit(solution)/shard_map/ppermute | solution.py:16
  111.6 0.6 copy-done.6
  112.3 0.6 multiply_reduce_fusion.7
  113.3 3.0 %collective-permute-done.2 = bf16[256,1024]{1,0:T(8,128)(2,1)} collective-permute-done((bf16[256,1024]{1,0:T(8,128)(2,1)}, bf16[256,1024]{1,0:T(8,128)(2,1)}, u32[]{:S(2)}, u32[]{:S(2)}) %collective-permute-start.2) | collective-permute-done | bytes 524320 | tf_op jit(solution)/shard_map/ppermute | solution.py:16
  116.3 3.8 %collective-permute-start.3 = (bf16[256,1024]{1,0:T(8,128)(2,1)}, bf16[256,1024]{1,0:T(8,128)(2,1)S(1)}, u32[]{:S(2)}, u32[]{:S(2)}) collective-permute-start(bf16[256,1024]{1,0:T(8,128)(2,1)} %collective-permute-done.2), channel_id=1, source_target_pairs={{0,28},{4,0},{8,4},{12,8},{16,12},{20,16},{24,20},{28,24},{1,29},{... | collective-permute-start | bytes 1572872 | tf_op jit(solution)/shard_map/ppermute | solution.py:16
  120.1 2.2 multiply_reduce_fusion.3
  122.7 16.0 %collective-permute-done.6 = f32[256,1024]{1,0:T(8,128)} collective-permute-done((f32[256,1024]{1,0:T(8,128)}, f32[256,1024]{1,0:T(8,128)}, u32[]{:S(2)}, u32[]{:S(2)}) %collective-permute-start.6) | collective-permute-done | bytes 1048608 | tf_op jit(solution)/shard_map/ppermute | solution.py:16
  138.8 1.4 add.242
  140.1 4.1 %collective-permute-start.7 = (f32[256,1024]{1,0:T(8,128)S(1)}, f32[256,1024]{1,0:T(8,128)S(1)}, u32[]{:S(2)}, u32[]{:S(2)}) collective-permute-start(f32[256,1024]{1,0:T(8,128)S(1)} %add.242), channel_id=1, source_target_pairs={{0,28},{4,0},{8,4},{12,8},{16,12},{20,16},{24,20},{28,24},{1,29},{... | collective-permute-start | bytes 3145736 | tf_op jit(solution)/shard_map/ppermute | solution.py:16
  144.2 1.4 convolution_add_fusion.4
  145.6 1.4 convolution_add_fusion.3
  146.9 3.0 %collective-permute-done.3 = bf16[256,1024]{1,0:T(8,128)(2,1)S(1)} collective-permute-done((bf16[256,1024]{1,0:T(8,128)(2,1)}, bf16[256,1024]{1,0:T(8,128)(2,1)S(1)}, u32[]{:S(2)}, u32[]{:S(2)}) %collective-permute-start.3) | collective-permute-done | bytes 524320 | tf_op jit(solution)/shard_map/ppermute | solution.py:16
  149.9 1.2 multiply_reduce_fusion.2
  151.4 20.2 %collective-permute-done.7 = f32[256,1024]{1,0:T(8,128)S(1)} collective-permute-done((f32[256,1024]{1,0:T(8,128)S(1)}, f32[256,1024]{1,0:T(8,128)S(1)}, u32[]{:S(2)}, u32[]{:S(2)}) %collective-permute-start.7) | collective-permute-done | bytes 1048608 | tf_op jit(solution)/shard_map/ppermute | solution.py:16
  171.9 1.4 convolution_add_fusion.2
  173.2 11.6 %fusion.63 = f32[3]{0:T(128)S(1)} fusion(f32[1]{0:T(128)} %bitcast.24, f32[1]{0:T(128)} %bitcast.23, f32[1]{0:T(128)} %bitcast.22, f32[1]{0:T(128)} %bitcast.27, f32[1]{0:T(128)} %bitcast.26, f32[1]{0:T(128)} %bitcast.25, f32[1]{0:T(128)} %bitcast.21, f32[1]{0:T(128)} %bitcast.20, f32[1]{0:T(128)} %bitcast.19, f32[1]{0:T(128)} %bitcast.18, f32[1]{0:T(128)} %bitcast.17, ...), kind=kLoop, calls=%fused_computation.151 | loop fusion | flops 51 | bytes 84 | tf_op jit(solution)/shard_map/add | solution.py:119
  184.8 0.5 multiply_reduce_fusion.1
  185.3 1.2 subtract_divide_fusion.1
  186.5 32.2 %collective-permute-done.8 = f32[256,1024]{1,0:T(8,128)S(1)} collective-permute-done((f32[256,1024]{1,0:T(8,128)S(1)}, f32[256,1024]{1,0:T(8,128)S(1)}, u32[]{:S(2)}, u32[]{:S(2)}) %collective-permute-start.8) | collective-permute-done | bytes 1048608 | tf_op jit(solution)/shard_map/ppermute | solution.py:16
  219.4 1.1 broadcast_multiply_fusion
  220.5 38.3 %all-reduce = (f32[1024]{0:T(1024)}, f32[3]{0:T(128)S(1)}) all-reduce(f32[1024]{0:T(1024)S(1)} %get-tuple-element.26, f32[3]{0:T(128)S(1)} %fusion.63), channel_id=1, replica_groups=mesh['dp'=8,'rep'=4] {'dp','rep'}, use_global_device_ids=true, to_apply=%region_12.13 | all-reduce | flops 1027 | bytes 8216 | tf_op jit(solution)/shard_map/psum | solution.py:136
  258.8 0.5 copy-done.7
  259.3 0.6 slice.14
  (52 shorter events, 5.4 us)
Async XLA Ops:
  1.6 22.7 %copy-start = (bf16[256,1024]{1,0:T(8,128)(2,1)S(1)}, bf16[256,1024]{1,0:T(8,128)(2,1)}, u32[]{:S(2)}) copy-start(bf16[256,1024]{1,0:T(8,128)(2,1)} %param.7) | copy-start | bytes 1572868
  19.4 4.9 %copy-start.2 = (f32[1024]{0:T(1024)S(1)}, f32[1024]{0:T(1024)}, u32[]{:S(2)}) copy-start(f32[1024]{0:T(1024)} %param.8) | copy-start | bytes 12292
  20.0 47.4 %all-to-all-start = ((s32[4,1,16]{2,1,0:T(1,128)}), s32[4,1,16]{2,1,0:T(1,128)S(1)}, u32[]{:S(2)}, u32[]{:S(2)}) async-start(s32[4,1,16]{2,1,0:T(1,128)} %bitcast.5), calls=%async_computation | async-start | bytes 4096 | tf_op jit(solution)/shard_map/all_to_all | solution.py:101
  24.5 5.3 %copy-start.1 = (bf16[256,1024]{1,0:T(8,128)(2,1)S(1)}, bf16[256,1024]{1,0:T(8,128)(2,1)}, u32[]{:S(2)}) copy-start(bf16[256,1024]{1,0:T(8,128)(2,1)} %param.6) | copy-start | bytes 1572868
  24.7 42.8 %collective-permute-start = (bf16[256,1024]{1,0:T(8,128)(2,1)S(1)}, bf16[256,1024]{1,0:T(8,128)(2,1)}, u32[]{:S(2)}, u32[]{:S(2)}) collective-permute-start(bf16[256,1024]{1,0:T(8,128)(2,1)S(1)} %fusion.77), channel_id=1, source_target_pairs={{0,28},{4,0},{8,4},{12,8},{16,12},{20,16},{24,20},{28,24},{1,29},{... | collective-permute-start | bytes 1572872 | tf_op jit(solution)/shard_map/ppermute | solution.py:16
  34.1 36.8 %collective-permute-start.4 = (f32[256,1024]{1,0:T(8,128)}, f32[256,1024]{1,0:T(8,128)}, u32[]{:S(2)}, u32[]{:S(2)}) collective-permute-start(f32[256,1024]{1,0:T(8,128)} %fusion.33), channel_id=1, source_target_pairs={{0,28},{4,0},{8,4},{12,8},{16,12},{20,16},{24,20},{28,24},{1,29},{... | collective-permute-start | bytes 3145736 | tf_op jit(solution)/shard_map/ppermute | solution.py:16
  50.4 0.5 copy-start.5
  67.5 15.1 %collective-permute-start.1 = (bf16[256,1024]{1,0:T(8,128)(2,1)}, bf16[256,1024]{1,0:T(8,128)(2,1)}, u32[]{:S(2)}, u32[]{:S(2)}) collective-permute-start(bf16[256,1024]{1,0:T(8,128)(2,1)} %collective-permute-done), channel_id=1, source_target_pairs={{0,28},{4,0},{8,4},{12,8},{16,12},{20,16},{24,20},{28,24},{1,29},{... | collective-permute-start | bytes 1572872 | tf_op jit(solution)/shard_map/ppermute | solution.py:16
  73.5 31.6 %collective-permute-start.5 = (f32[256,1024]{1,0:T(8,128)}, f32[256,1024]{1,0:T(8,128)}, u32[]{:S(2)}, u32[]{:S(2)}) collective-permute-start(f32[256,1024]{1,0:T(8,128)} %convolution_add_fusion), channel_id=1, source_target_pairs={{0,28},{4,0},{8,4},{12,8},{16,12},{20,16},{24,20},{28,24},{1,29},{... | collective-permute-start | bytes 3145736 | tf_op jit(solution)/shard_map/ppermute | solution.py:16
  76.4 34.8 %all-to-all-start.1 = ((bf16[4,16,1024]{2,1,0:T(8,128)(2,1)}), bf16[4,16,1024]{2,1,0:T(8,128)(2,1)S(1)}, u32[]{:S(2)}, u32[]{:S(2)}) async-start(bf16[4,16,1024]{2,1,0:T(8,128)(2,1)} %broadcast_select_fusion), calls=%async_computation.1 | async-start | bytes 262144 | tf_op jit(solution)/shard_map/all_to_all | solution.py:103
  85.2 31.1 %collective-permute-start.2 = (bf16[256,1024]{1,0:T(8,128)(2,1)}, bf16[256,1024]{1,0:T(8,128)(2,1)}, u32[]{:S(2)}, u32[]{:S(2)}) collective-permute-start(bf16[256,1024]{1,0:T(8,128)(2,1)} %collective-permute-done.1), channel_id=1, source_target_pairs={{0,28},{4,0},{8,4},{12,8},{16,12},{20,16},{24,20},{28,24},{1,29},{... | collective-permute-start | bytes 1572872 | tf_op jit(solution)/shard_map/ppermute | solution.py:16
  107.4 3.9 %copy-start.3 = (pred[64]{0:T(512)(128)(4,1)S(1)}, pred[64]{0:T(512)(128)(4,1)}, u32[]{:S(2)}) copy-start(pred[64]{0:T(512)(128)(4,1)} %broadcast_compare_fusion.2) | copy-start | bytes 196
  107.4 3.9 %copy-start.4 = (s32[64]{0:T(128)S(1)}, s32[64]{0:T(128)}, u32[]{:S(2)}) copy-start(s32[64]{0:T(128)} %scatter_custom_fusion) | copy-start | bytes 772
  107.4 31.4 %collective-permute-start.6 = (f32[256,1024]{1,0:T(8,128)}, f32[256,1024]{1,0:T(8,128)}, u32[]{:S(2)}, u32[]{:S(2)}) collective-permute-start(f32[256,1024]{1,0:T(8,128)} %add.241), channel_id=1, source_target_pairs={{0,28},{4,0},{8,4},{12,8},{16,12},{20,16},{24,20},{28,24},{1,29},{... | collective-permute-start | bytes 3145736 | tf_op jit(solution)/shard_map/ppermute | solution.py:16
  111.6 0.6 copy-start.6
  116.3 33.6 %collective-permute-start.3 = (bf16[256,1024]{1,0:T(8,128)(2,1)}, bf16[256,1024]{1,0:T(8,128)(2,1)S(1)}, u32[]{:S(2)}, u32[]{:S(2)}) collective-permute-start(bf16[256,1024]{1,0:T(8,128)(2,1)} %collective-permute-done.2), channel_id=1, source_target_pairs={{0,28},{4,0},{8,4},{12,8},{16,12},{20,16},{24,20},{28,24},{1,29},{... | collective-permute-start | bytes 1572872 | tf_op jit(solution)/shard_map/ppermute | solution.py:16
  140.1 31.5 %collective-permute-start.7 = (f32[256,1024]{1,0:T(8,128)S(1)}, f32[256,1024]{1,0:T(8,128)S(1)}, u32[]{:S(2)}, u32[]{:S(2)}) collective-permute-start(f32[256,1024]{1,0:T(8,128)S(1)} %add.242), channel_id=1, source_target_pairs={{0,28},{4,0},{8,4},{12,8},{16,12},{20,16},{24,20},{28,24},{1,29},{... | collective-permute-start | bytes 3145736 | tf_op jit(solution)/shard_map/ppermute | solution.py:16
  171.8 46.9 %collective-permute-start.8 = (f32[256,1024]{1,0:T(8,128)S(1)}, f32[256,1024]{1,0:T(8,128)S(1)}, u32[]{:S(2)}, u32[]{:S(2)}) collective-permute-start(f32[256,1024]{1,0:T(8,128)S(1)} %add.243), channel_id=1, source_target_pairs={{0,16},{4,20},{8,24},{12,28},{16,0},{20,4},{24,8},{28,12},{1,17},{... | collective-permute-start | bytes 3145736 | tf_op jit(solution)/shard_map/ppermute | solution.py:16
  258.8 0.5 copy-start.7
where the time goes:
time: 264 us; the launch traced here: 262 us
  waiting for transfers between devices  93.2 us (35%)
  local copies, waits for them, and re-layouts  51.8 us (20%)
  blocking collectives  38.3 us (15%)
  starting transfers between devices  31.1 us (12%)
  other arithmetic  23.6 us (9%)
  matrix products  19.7 us (7%)
  between operations  4.01 us (2%)
    ppermute x9, waiting for transfers between devices, shifted(): return lax.ppermute(value, axis, pairs)  93.1 us
    psum x1, blocking collectives, per_device(): gain_total, summary_total = lax.psum((gain_part, summary), ('dp', 'rep'))  38.3 us
    ppermute x9, starting transfers between devices, shifted(): return lax.ppermute(value, axis, pairs)  23.5 us
    scatter x1, local copies, waits for them, and re-layouts, per_device(): slot_pair = jnp.zeros((slot_total,), jnp.int32).at[target].set(jnp.arange...  16 us
    scatter x1, local copies, waits for them, and re-layouts, per_device(): asked_rows = jnp.zeros((slot_total,), jnp.int32).at[target].set(row_withi...  15.5 us
    scatter x1, local copies, waits for them, and re-layouts, per_device(): jnp.zeros((slot_total,), jnp.float32).at[target].set(1.0, mode='drop')  15.5 us
    add x1, other arithmetic, per_device(): summary + jnp.stack([jnp.sum(hard_weights * hard_products * multiplier),...  11.6 us
    dot_general x5, matrix products, score_tile(): lax.dot_general(circ_block, rec_block, (((1,), (1,)), ((), ())), preferre...  9.19 us
  transfers between devices with their start and end apart: 11, of which 7 were waited for; matrix products, arithmetic and copies ran while one was open for 27% of the time, Pallas kernels for 0%

commit v1 on v0

--- a/solution.py
+++ b/solution.py
@@ -4,7 +4,6 @@
 from jax.sharding import PartitionSpec as P
 
 HOPS = 4
-CAP = 16
 
 
 EPSILON = 1e-06
@@ -49,6 +48,13 @@
     return (weights.astype(jnp.bfloat16), summary)
 
 
+def tile_terms(circ_block, rec_block, multiplier, bias_value):
+    products = lax.dot_general(
+        circ_block, rec_block, (((1,), (1,)), ((), ())), preferred_element_type=jnp.float32
+    )
+    return products * multiplier + bias_value
+
+
 def per_device(circuits, records, record_gain, log_scale, logit_bias, hard_ids):
     pair_rows = circuits.shape[0]
     list_width = hard_ids.shape[1]
@@ -61,66 +67,47 @@
     rec_emb = rec_unit.astype(jnp.bfloat16)
     multiplier = jnp.exp(log_scale[0])
     bias_value = logit_bias[0]
+    even = lax.axis_index("dp") % 2 == 0
+    swap = [(source, source ^ 1) for source in range(loop_count)]
+
+    rec2 = shifted(rec_emb, "dp", -2)
+    circ2 = shifted(circ_emb, "dp", 2)
+    rec4 = shifted(rec2, "dp", -2)
+    circ4 = shifted(circ2, "dp", 2)
+    rec1 = lax.ppermute(jnp.where(even, rec2, rec_emb), "dp", swap)
+    circ1 = lax.ppermute(jnp.where(even, circ_emb, circ2), "dp", swap)
+    rec3 = lax.ppermute(jnp.where(even, rec4, rec2), "dp", swap)
+    circ3 = lax.ppermute(jnp.where(even, circ2, circ4), "dp", swap)
+
     own_weights, summary = score_tile(circ_emb, rec_emb, multiplier, bias_value, True)
     grad_circ = jnp.dot(own_weights, rec_emb, preferred_element_type=jnp.float32)
-    running = transposed_product(own_weights, circ_emb)
-    visitor = rec_emb
-    for hop_index in range(HOPS):
-        visitor = shifted(visitor, "dp", -1)
-        running = shifted(running, "dp", -1)
+    grad_rec = transposed_product(own_weights, circ_emb)
+
+    everyone = lax.all_gather(rec_emb, "rep", axis=0, tiled=True)
+    first_row = (lax.axis_index("dp") * rep_count) * pair_rows
+    columns = lax.broadcasted_iota(jnp.int32, (pair_rows, rep_count * pair_rows), 1) + first_row
+    times = jnp.zeros(columns.shape, jnp.float32)
+    for entry in range(list_width):
+        times = times + (hard_ids[:, entry][:, None] == columns).astype(jnp.float32)
+
+    for visitor, guest in ((rec2, circ2), (rec1, circ1), (rec4, circ4), (rec3, circ3)):
         weights, portion = score_tile(circ_emb, visitor, multiplier, bias_value, False)
         grad_circ = grad_circ + jnp.dot(weights, visitor, preferred_element_type=jnp.float32)
         summary = summary + portion
-        running = running + transposed_product(weights, circ_emb)
-    grad_rec = shifted(running, "dp", HOPS)
-    entry_ids = hard_ids.reshape(-1)
-    entry_count = entry_ids.shape[0]
-    is_live = entry_ids >= 0
-    owner_dev = entry_ids // pair_rows % rep_count
-    row_within = entry_ids % pair_rows
-    owner_hits = (
-        (owner_dev[:, None] == jnp.arange(rep_count, dtype=jnp.int32)[None, :]) & is_live[:, None]
-    ).astype(jnp.int32)
-    before = jnp.cumsum(owner_hits, axis=0) - owner_hits
-    slot_index = jnp.sum(before * owner_hits, axis=1)
-    slot_total = rep_count * CAP
-    target = jnp.where(is_live, owner_dev * CAP + slot_index, slot_total)
-    asked_rows = (
-        jnp.zeros((slot_total,), jnp.int32)
-        .at[target]
-        .set(row_within, mode="drop")
-        .reshape(rep_count, CAP)
-    )
-    slot_pair = (
-        jnp.zeros((slot_total,), jnp.int32)
-        .at[target]
-        .set(jnp.arange(entry_count, dtype=jnp.int32) // list_width, mode="drop")
-    )
-    slot_live = jnp.zeros((slot_total,), jnp.float32).at[target].set(1.0, mode="drop")
-    found_rows = jnp.take(
-        rec_emb, lax.all_to_all(asked_rows, "rep", split_axis=0, concat_axis=0, tiled=True), axis=0
-    )
-    fetched = lax.all_to_all(found_rows, "rep", split_axis=0, concat_axis=0, tiled=True)
-    fetched = fetched.reshape(slot_total, fetched.shape[2])
-    slot_products = lax.dot_general(
-        fetched, circ_emb, (((1,), (1,)), ((), ())), preferred_element_type=jnp.float32
-    )
-    chosen = (slot_pair[:, None] == lax.broadcasted_iota(jnp.int32, (slot_total, pair_rows), 1)) & (
-        slot_live[:, None] > 0
-    )
-    hard_products = jnp.sum(jnp.where(chosen, slot_products, 0.0), axis=1)
-    hard_scores = hard_products * multiplier + bias_value
-    hard_weights = jnp.where(slot_live > 0, jax.nn.sigmoid(hard_scores), 0.0)
-    hard_losses = jnp.where(slot_live > 0, jax.nn.softplus(hard_scores), 0.0)
-    spread = jnp.where(
-        chosen, hard_weights.astype(jnp.bfloat16)[:, None], jnp.zeros((), jnp.bfloat16)
-    )
-    hard_grad = transposed_product(spread, fetched)
+        scores = tile_terms(guest, rec_emb, multiplier, bias_value)
+        weights = jax.nn.sigmoid(scores).astype(jnp.bfloat16)
+        grad_rec = grad_rec + transposed_product(weights, guest)
+
+    scores = tile_terms(circ_emb, everyone, multiplier, bias_value)
+    sigmoids = jax.nn.sigmoid(scores)
+    weights = times * sigmoids
+    narrow = (times * sigmoids.astype(jnp.bfloat16).astype(jnp.float32)).astype(jnp.bfloat16)
+    hard_grad = jnp.dot(narrow, everyone, preferred_element_type=jnp.float32)
     summary = summary + jnp.stack(
         [
-            jnp.sum(hard_weights * hard_products * multiplier),
-            jnp.sum(hard_weights),
-            jnp.sum(hard_losses),
+            jnp.sum(weights * (scores - bias_value)),
+            jnp.sum(weights),
+            jnp.sum(times * jax.nn.softplus(scores)),
         ]
     )
     grad_circ_emb = multiplier * (grad_circ + hard_grad)

time: 264 us -> 179 us (0.68)
  local copies, waits for them, and re-layouts: 51.8 us -> 1.44 us
  waiting for transfers between devices: 93.2 us -> 48.6 us
  matrix products: 19.7 us -> 36.1 us
  starting transfers between devices: 31.1 us -> 15.7 us
  between operations: 4.01 us -> 17.4 us
  other arithmetic: 23.6 us -> 20.3 us
    ppermute x9 -> x4, waiting for transfers between devices: 93.1 us -> 24.2 us  [shifted(): return lax.ppermute(value, axis, pairs)]
    scatter x3 -> x0, local copies, waits for them, and re-layouts: 47 us -> none  [the longest x1 16 us: per_device(): slot_pair = jnp.zeros((slot_total,), jnp.int32).at[target].set(jnp.arange...]
    ppermute x0 -> x4, waiting for transfers between devices: none -> 24.4 us  [the longest x1 10 us: per_device(): circ3 = lax.ppermute(jnp.where(even, circ2, circ4), 'dp', swap)]
    ppermute x9 -> x4, starting transfers between devices: 23.5 us -> 11 us  [shifted(): return lax.ppermute(value, axis, pairs)]
    dot_general x1 -> x2, matrix products: 0.38 us -> 9.2 us  [the longest x1 5.15 us: tile_terms(): lax.dot_general(circ_block, rec_block, (((1,), (1,)), ((), ())), preferre...]
    all_to_all x2 -> x0, starting transfers between devices: 7.53 us -> none  [the longest x1 4.21 us: per_device(): lax.all_to_all(asked_rows, 'rep', split_axis=0, concat_axis=0, tiled=True)]
    dot_general x6 -> x5, matrix products: 5.31 us -> 12.3 us  [transposed_product(): lax.dot_general(left, right, (((0,), (0,)), ((), ())), preferred_element_...]
    ppermute x0 -> x4, starting transfers between devices: none -> 4.68 us  [the longest x1 2.56 us: per_device(): circ3 = lax.ppermute(jnp.where(even, circ2, circ4), 'dp', swap)]
  transfers between devices with their start and end apart: 11 -> 9, of which waited for: 7 -> 7; matrix products, arithmetic and copies ran while one was open for 27% -> 17% of each run, Pallas kernels for 0% -> 0%
where the time goes in v1:
time: 179 us
  waiting for transfers between devices  48.6 us (27%)
  blocking collectives  39.1 us (22%)
  matrix products  36.1 us (20%)
  other arithmetic  20.3 us (11%)
  between operations  17.4 us (10%)
  starting transfers between devices  15.7 us (9%)
    psum x1, blocking collectives, per_device(): gain_total, summary_total = lax.psum((gain_part, summary), ('dp', 'rep'))  39.1 us
    ppermute x4, waiting for transfers between devices, shifted(): return lax.ppermute(value, axis, pairs)  24.2 us
    dot_general x5, matrix products, transposed_product(): lax.dot_general(left, right, (((0,), (0,)), ((), ())), preferred_element_...  12.3 us
    add x1, other arithmetic, per_device(): summary + jnp.stack([jnp.sum(weights * (scores - bias_value)), jnp.sum(we...  11.1 us
    ppermute x4, starting transfers between devices, shifted(): return lax.ppermute(value, axis, pairs)  11 us
    ppermute x1, waiting for transfers between devices, per_device(): circ3 = lax.ppermute(jnp.where(even, circ2, circ4), 'dp', swap)  10 us
    dot_general x5, matrix products, score_tile(): lax.dot_general(circ_block, rec_block, (((1,), (1,)), ((), ())), preferre...  8.68 us
    ppermute x1, waiting for transfers between devices, per_device(): rec1 = lax.ppermute(jnp.where(even, rec2, rec_emb), 'dp', swap)  8.29 us
  transfers between devices with their start and end apart: 9, of which 7 were waited for; matrix products, arithmetic and copies ran while one was open for 17% of the time, Pallas kernels for 0%

profile of v1, /device:TPU:0, one launch (start us, length us, event | category | flops | bytes accessed | tf_op | source)
XLA Modules:
  0.0 178.6 jit_solution(16136791953172690187)
XLA Ops:
  7.2 0.0 all-gather.2.cloned.1.call-start
  7.2 1.3 fusion.38
  8.6 2.0 %fusion.84 = bf16[256,1024]{1,0:T(8,128)(2,1)} fusion(f32[256]{0:T(256)S(1)} %add_sqrt_fusion, f32[1024]{0:T(1024)} %param.8, bf16[256,1024]{1,0:T(8,128)(2,1)} %param.7), kind=kLoop, calls=%fused_computation.140 | loop fusion | flops 1048576 | bytes 1053696 | tf_op jit(solution)/shard_map/convert_element_type | solution.py:67
  10.6 0.0 all-gather.2.cloned.1.call-update
  10.6 5.1 %collective-permute-start = (bf16[256,1024]{1,0:T(8,128)(2,1)}, bf16[256,1024]{1,0:T(8,128)(2,1)}, u32[]{:S(2)}, u32[]{:S(2)}) collective-permute-start(bf16[256,1024]{1,0:T(8,128)(2,1)} %fusion.84), channel_id=1, source_target_pairs={{0,24},{4,28},{8,0},{12,4},{16,8},{20,12},{24,16},{28,20},{1,25},{... | collective-permute-start | bytes 1572872 | tf_op jit(solution)/shard_map/ppermute | solution.py:15
  15.7 0.2 fusion.39
  15.9 0.2 fusion.83
  16.2 0.1 collective-permute-start.4
  17.7 1.2 multiply_reduce_fusion.8
  18.9 0.3 fusion.70
  19.2 1.3 fusion.68
  20.5 7.8 %collective-permute-done = bf16[256,1024]{1,0:T(8,128)(2,1)} collective-permute-done((bf16[256,1024]{1,0:T(8,128)(2,1)}, bf16[256,1024]{1,0:T(8,128)(2,1)}, u32[]{:S(2)}, u32[]{:S(2)}) %collective-permute-start) | collective-permute-done | bytes 524320 | tf_op jit(solution)/shard_map/ppermute | solution.py:15
  28.4 4.3 %collective-permute-start.2 = (bf16[256,1024]{1,0:T(8,128)(2,1)}, bf16[256,1024]{1,0:T(8,128)(2,1)}, u32[]{:S(2)}, u32[]{:S(2)}) collective-permute-start(bf16[256,1024]{1,0:T(8,128)(2,1)} %collective-permute-done), channel_id=1, source_target_pairs={{0,24},{4,28},{8,0},{12,4},{16,8},{20,12},{24,16},{28,20},{1,25},{... | collective-permute-start | bytes 1572872 | tf_op jit(solution)/shard_map/ppermute | solution.py:15
  32.6 7.8 %collective-permute-done.4 = bf16[256,1024]{1,0:T(8,128)(2,1)S(1)} collective-permute-done((bf16[256,1024]{1,0:T(8,128)(2,1)S(1)}, bf16[256,1024]{1,0:T(8,128)(2,1)S(1)}, u32[]{:S(2)}, u32[]{:S(2)}) %collective-permute-start.4) | collective-permute-done | bytes 524320 | tf_op jit(solution)/shard_map/ppermute | solution.py:15
  40.4 1.5 collective-permute-start.6
  42.0 3.1 %convolution_add_fusion.2 = f32[256,1024]{1,0:T(8,128)} fusion(f32[256,1024]{1,0:T(8,128)} %fusion.68, bf16[256,1024]{1,0:T(8,128)(2,1)S(1)} %collective-permute-done.4, bf16[256,1024]{1,0:T(8,128)(2,1)S(1)} %copy-done, f32[]{:T(128)} %bitcast.69, f32[]{:T(128)} %bitcast), kind=kOutput, calls=%fused_computation.5 | convolution fusion | flops 269090816 | bytes 3145736 | tf_op jit(solution)/shard_map/dot_general | solution.py:25
  45.1 2.2 %multiply_reduce_fusion.7 = (f32[]{:T(128)}, f32[]{:T(128)}, f32[]{:T(128)}, f32[256,256]{1,0:T(8,128)S(1)}) fusion(f32[]{:T(128)} %bitcast.74, f32[]{:T(128)} %bitcast, bf16[256,1024]{1,0:T(8,128)(2,1)S(1)} %fusion.83, bf16[256,1024]{1,0:T(8,128)(2,1)} %collective-permute-done), kind=kOutput, calls=%fused_computation.94 | convolution fusion | flops 135266304 | bytes 1310740 | tf_op jit(solution)/shard_map/dot_general | solution.py:31
  47.3 2.4 %convolution_add_fusion.5 = f32[256,1024]{1,0:T(8,128)} fusion(f32[256,1024]{1,0:T(8,128)S(1)} %fusion.70, bf16[256,1024]{1,0:T(8,128)(2,1)} %collective-permute-done, f32[256,256]{1,0:T(8,128)S(1)} %get-tuple-element.55), kind=kOutput, calls=%fused_computation.11 | convolution fusion | flops 134742016 | bytes 2883584 | tf_op jit(solution)/shard_map/dot_general | solution.py:95
  49.7 1.9 %collective-permute-done.2 = bf16[256,1024]{1,0:T(8,128)(2,1)} collective-permute-done((bf16[256,1024]{1,0:T(8,128)(2,1)}, bf16[256,1024]{1,0:T(8,128)(2,1)}, u32[]{:S(2)}, u32[]{:S(2)}) %collective-permute-start.2) | collective-permute-done | bytes 524320 | tf_op jit(solution)/shard_map/ppermute | solution.py:15
  51.6 1.6 broadcast_select_fusion.3
  53.2 1.4 collective-permute-start.3
  54.6 0.7 collective-permute-start.1
  55.3 6.6 %collective-permute-done.6 = bf16[256,1024]{1,0:T(8,128)(2,1)} collective-permute-done((bf16[256,1024]{1,0:T(8,128)(2,1)S(1)}, bf16[256,1024]{1,0:T(8,128)(2,1)}, u32[]{:S(2)}, u32[]{:S(2)}) %collective-permute-start.6) | collective-permute-done | bytes 524320 | tf_op jit(solution)/shard_map/ppermute | solution.py:15
  61.9 1.2 broadcast_select_fusion.1
  63.0 2.6 %collective-permute-start.7 = (bf16[256,1024]{1,0:T(8,128)(2,1)S(1)}, bf16[256,1024]{1,0:T(8,128)(2,1)S(1)}, u32[]{:S(2)}, u32[]{:S(2)}) collective-permute-start(bf16[256,1024]{1,0:T(8,128)(2,1)S(1)} %get-tuple-element.28), channel_id=1, source_target_pairs={{0,4},{4,0},{8,12},{12,8},{16,20},{20,16},{24,28},{28,24},{1,5},{5... | collective-permute-start | bytes 1572872 | tf_op jit(solution)/shard_map/ppermute | solution.py:80
  65.6 0.0 collective-permute-start.5
  65.6 2.9 %multiply_reduce_fusion.5 = (f32[]{:T(128)}, f32[]{:T(128)}, f32[]{:T(128)}, f32[256,256]{1,0:T(8,128)}) fusion(f32[]{:T(128)} %bitcast.72, f32[]{:T(128)} %bitcast, bf16[256,1024]{1,0:T(8,128)(2,1)S(1)} %copy-done.6, bf16[256,1024]{1,0:T(8,128)(2,1)} %collective-permute-done.2), kind=kOutput, calls=%fused_computation.92 | convolution fusion | flops 135266304 | bytes 1310740 | tf_op jit(solution)/shard_map/dot_general | solution.py:31
  68.6 1.2 multiply_reduce_fusion.4
  69.7 1.3 fusion.51
  71.0 8.3 %collective-permute-done.1 = bf16[256,1024]{1,0:T(8,128)(2,1)S(1)} collective-permute-done((bf16[256,1024]{1,0:T(8,128)(2,1)S(1)}, bf16[256,1024]{1,0:T(8,128)(2,1)S(1)}, u32[]{:S(2)}, u32[]{:S(2)}) %collective-permute-start.1) | collective-permute-done | bytes 524320 | tf_op jit(solution)/shard_map/ppermute | solution.py:77
  79.3 1.2 multiply_reduce_fusion.6
  80.5 10.0 %collective-permute-done.7 = bf16[256,1024]{1,0:T(8,128)(2,1)S(1)} collective-permute-done((bf16[256,1024]{1,0:T(8,128)(2,1)S(1)}, bf16[256,1024]{1,0:T(8,128)(2,1)S(1)}, u32[]{:S(2)}, u32[]{:S(2)}) %collective-permute-start.7) | collective-permute-done | bytes 524320 | tf_op jit(solution)/shard_map/ppermute | solution.py:80
  90.6 0.8 copy-done.13
  91.3 3.1 %fusion.37 = f32[256,1024]{1,0:T(8,128)} fusion(bf16[256,1024]{1,0:T(8,128)(2,1)} %copy-done.13, bf16[256,1024]{1,0:T(8,128)(2,1)S(1)} %copy-done, f32[]{:T(128)} %bitcast.76, f32[]{:T(128)} %bitcast), kind=kOutput, calls=%fused_computation.58 | convolution fusion | flops 268828672 | bytes 2097160 | tf_op jit(solution)/shard_map/dot_general | solution.py:25
  94.4 6.1 %collective-permute-done.5 = bf16[256,1024]{1,0:T(8,128)(2,1)S(1)} collective-permute-done((bf16[256,1024]{1,0:T(8,128)(2,1)}, bf16[256,1024]{1,0:T(8,128)(2,1)S(1)}, u32[]{:S(2)}, u32[]{:S(2)}) %collective-permute-start.5) | collective-permute-done | bytes 524320 | tf_op jit(solution)/shard_map/ppermute | solution.py:78
  100.5 1.9 %convolution_add_fusion.1 = f32[256,1024]{1,0:T(8,128)} fusion(f32[256,1024]{1,0:T(8,128)S(1)} %copy-done.4, bf16[256,1024]{1,0:T(8,128)(2,1)S(1)} %collective-permute-done.5, bf16[256,1024]{1,0:T(8,128)(2,1)S(1)} %copy-done, f32[]{:T(128)} %bitcast.68, f32[]{:T(128)} %bitcast), kind=kOutput, calls=%fused_computation.4 | convolution fusion | flops 269090816 | bytes 3145736 | tf_op jit(solution)/shard_map/dot_general | solution.py:25
  102.4 2.9 %multiply_reduce_fusion.1 = (f32[256]{0:T(256)S(1)}, f32[256,1024]{1,0:T(8,128)S(1)}) fusion(f32[256]{0:T(256)S(1)} %add_sqrt_fusion, f32[1024]{0:T(1024)S(1)} %copy-done.11, bf16[256,1024]{1,0:T(8,128)(2,1)S(1)} %copy-done.1, f32[256,1024]{1,0:T(8,128)} %fusion.37, f32[256,1024]{1,0:T(8,128)} %convolution_add_fusion.1, ...), kind=kOutput, calls=%fused_computation.66 | convolution fusion | flops 270925568 | bytes 4724744 | tf_op jit(solution)/shard_map/dot_general | solution.py:25
  105.3 0.4 fusion.40
  105.6 1.1 broadcast_multiply_fusion
  106.7 0.3 convolution_add_fusion.4
  107.1 0.0 all-gather.2.cloned.1.call-done
  107.1 5.2 %multiply_reduce_fusion = (f32[]{:T(128)}, f32[]{:T(128)}, f32[]{:T(128)}, f32[256,1024]{1,0:T(8,128)S(1)}) fusion(f32[]{:T(128)} %bitcast.70, s32[256]{0:T(256)S(1)} %bitcast.106, s32[256]{0:T(256)S(1)} %bitcast.108, s32[256]{0:T(256)S(1)} %bitcast.80, s32[256]{0:T(256)S(1)} %bitcast.82, s32[256]{0:T(256)S(1)} %bitcast.84, s32[256]{0:T(256)S(1)} %bitcast.86, ...), kind=kOutput, calls=%fused_computation.64 | convolution fusion | flops 553910272 | bytes 3690516 | tf_op jit(solution)/shard_map/dot_general | solution.py:52
  112.3 11.1 %fusion.74 = f32[3]{0:T(128)S(1)} fusion(f32[1]{0:T(128)} %bitcast.32, f32[1]{0:T(128)} %bitcast.31, f32[1]{0:T(128)} %bitcast.30, f32[1]{0:T(128)} %bitcast.35, f32[1]{0:T(128)} %bitcast.34, f32[1]{0:T(128)} %bitcast.33, f32[1]{0:T(128)} %bitcast.29, f32[1]{0:T(128)} %bitcast.28, f32[1]{0:T(128)} %bitcast.27, f32[1]{0:T(128)} %bitcast.26, f32[1]{0:T(128)} %bitcast.25, ...), kind=kLoop, calls=%fused_computation.130 | loop fusion | flops 51 | bytes 84 | tf_op jit(solution)/shard_map/add | solution.py:106
  123.4 39.1 %all-reduce = (f32[1024]{0:T(1024)}, f32[3]{0:T(128)S(1)}) all-reduce(f32[1024]{0:T(1024)S(1)} %get-tuple-element.25, f32[3]{0:T(128)S(1)} %fusion.74), channel_id=1, replica_groups=mesh['dp'=8,'rep'=4] {'dp','rep'}, use_global_device_ids=true, to_apply=%region_5.6 | all-reduce | flops 1027 | bytes 8216 | tf_op jit(solution)/shard_map/psum | solution.py:123
  162.5 0.6 slice.70
  163.1 4.0 %fusion.43 = f32[256,1024]{1,0:T(8,128)S(1)} fusion(bf16[1024,1024]{1,0:T(8,128)(2,1)} %all-gather.2.cloned.1.call-done, f32[256,1024]{1,0:T(8,128)S(1)} %get-tuple-element.52, s32[1024]{0:T(1024)S(1)} %iota_add_fusion, s32[256]{0:T(256)S(1)} %bitcast.107, s32[256]{0:T(256)S(1)} %bitcast.109, s32[256]{0:T(256)S(1)} %bitcast.81, s32[256]{0:T(256)S(1)} %bitcast.83, ...), kind=kOutput, calls=%fused_computation.77 | convolution fusion | flops 551026688 | bytes 4214784 | tf_op jit(solution)/shard_map/dot_general | solution.py:105
  167.2 1.6 multiply_reduce_fusion.2
  168.8 1.2 subtract_divide_fusion.1
  (36 shorter events, 0.1 us)
Async XLA Ops:
  7.2 8.6 %copy-start.2 = (bf16[256,1024]{1,0:T(8,128)(2,1)S(1)}, bf16[256,1024]{1,0:T(8,128)(2,1)}, u32[]{:S(2)}) copy-start(bf16[256,1024]{1,0:T(8,128)(2,1)} %param.6) | copy-start | bytes 1572868
  7.2 9.7 %copy-start.12 = (s32[256,16]{0,1:T(8,128)S(1)}, s32[256,16]{0,1:T(8,128)}, u32[]{:S(2)}) copy-start(s32[256,16]{0,1:T(8,128)} %param.11) | copy-start | bytes 49156
  7.2 99.9 %all-gather.2.cloned.1.call-start = ((), (), s32[]{:S(2)}) async-start(), calls=%async_computation | async-start | bytes 2621440 | tf_op jit(solution)/shard_map/all_gather | solution.py:86
  10.6 7.1 %copy-start = (bf16[256,1024]{1,0:T(8,128)(2,1)S(1)}, bf16[256,1024]{1,0:T(8,128)(2,1)}, u32[]{:S(2)}) copy-start(bf16[256,1024]{1,0:T(8,128)(2,1)} %fusion.84) | copy-start | bytes 1572868
  10.6 17.7 %collective-permute-start = (bf16[256,1024]{1,0:T(8,128)(2,1)}, bf16[256,1024]{1,0:T(8,128)(2,1)}, u32[]{:S(2)}, u32[]{:S(2)}) collective-permute-start(bf16[256,1024]{1,0:T(8,128)(2,1)} %fusion.84), channel_id=1, source_target_pairs={{0,24},{4,28},{8,0},{12,4},{16,8},{20,12},{24,16},{28,20},{1,25},{... | collective-permute-start | bytes 1572872 | tf_op jit(solution)/shard_map/ppermute | solution.py:15
  16.1 28.9 %copy-start.5 = (bf16[256,1024]{1,0:T(8,128)(2,1)}, bf16[256,1024]{1,0:T(8,128)(2,1)S(1)}, u32[]{:S(2)}) copy-start(bf16[256,1024]{1,0:T(8,128)(2,1)S(1)} %fusion.83) | copy-start | bytes 1572868
  16.2 24.3 %collective-permute-start.4 = (bf16[256,1024]{1,0:T(8,128)(2,1)S(1)}, bf16[256,1024]{1,0:T(8,128)(2,1)S(1)}, u32[]{:S(2)}, u32[]{:S(2)}) collective-permute-start(bf16[256,1024]{1,0:T(8,128)(2,1)S(1)} %fusion.83), channel_id=1, source_target_pairs={{0,8},{4,12},{8,16},{12,20},{16,24},{20,28},{24,0},{28,4},{1,9},{5... | collective-permute-start | bytes 1572872 | tf_op jit(solution)/shard_map/ppermute | solution.py:15
  28.4 23.2 %collective-permute-start.2 = (bf16[256,1024]{1,0:T(8,128)(2,1)}, bf16[256,1024]{1,0:T(8,128)(2,1)}, u32[]{:S(2)}, u32[]{:S(2)}) collective-permute-start(bf16[256,1024]{1,0:T(8,128)(2,1)} %collective-permute-done), channel_id=1, source_target_pairs={{0,24},{4,28},{8,0},{12,4},{16,8},{20,12},{24,16},{28,20},{1,25},{... | collective-permute-start | bytes 1572872 | tf_op jit(solution)/shard_map/ppermute | solution.py:15
  40.4 21.4 %collective-permute-start.6 = (bf16[256,1024]{1,0:T(8,128)(2,1)S(1)}, bf16[256,1024]{1,0:T(8,128)(2,1)}, u32[]{:S(2)}, u32[]{:S(2)}) collective-permute-start(bf16[256,1024]{1,0:T(8,128)(2,1)S(1)} %collective-permute-done.4), channel_id=1, source_target_pairs={{0,8},{4,12},{8,16},{12,20},{16,24},{20,28},{24,0},{28,4},{1,9},{5... | collective-permute-start | bytes 1572872 | tf_op jit(solution)/shard_map/ppermute | solution.py:15
  47.3 4.3 %copy-start.1 = (bf16[256,1024]{1,0:T(8,128)(2,1)S(1)}, bf16[256,1024]{1,0:T(8,128)(2,1)}, u32[]{:S(2)}) copy-start(bf16[256,1024]{1,0:T(8,128)(2,1)} %param.7) | copy-start | bytes 1572868
  47.3 4.3 %copy-start.11 = (f32[1024]{0:T(1024)S(1)}, f32[1024]{0:T(1024)}, u32[]{:S(2)}) copy-start(f32[1024]{0:T(1024)} %param.8) | copy-start | bytes 12292
  49.7 16.0 %copy-start.6 = (bf16[256,1024]{1,0:T(8,128)(2,1)S(1)}, bf16[256,1024]{1,0:T(8,128)(2,1)}, u32[]{:S(2)}) copy-start(bf16[256,1024]{1,0:T(8,128)(2,1)} %copy-done.5) | copy-start | bytes 1572868
  53.2 15.4 %collective-permute-start.3 = (bf16[256,1024]{1,0:T(8,128)(2,1)S(1)}, bf16[256,1024]{1,0:T(8,128)(2,1)S(1)}, u32[]{:S(2)}, u32[]{:S(2)}) collective-permute-start(bf16[256,1024]{1,0:T(8,128)(2,1)S(1)} %get-tuple-element.30), channel_id=1, source_target_pairs={{0,4},{4,0},{8,12},{12,8},{16,20},{20,16},{24,28},{28,24},{1,5},{5... | collective-permute-start | bytes 1572872 | tf_op jit(solution)/shard_map/ppermute | solution.py:79
  54.6 24.7 %collective-permute-start.1 = (bf16[256,1024]{1,0:T(8,128)(2,1)S(1)}, bf16[256,1024]{1,0:T(8,128)(2,1)S(1)}, u32[]{:S(2)}, u32[]{:S(2)}) collective-permute-start(bf16[256,1024]{1,0:T(8,128)(2,1)S(1)} %get-tuple-element.29), channel_id=1, source_target_pairs={{0,4},{4,0},{8,12},{12,8},{16,20},{20,16},{24,28},{28,24},{1,5},{5... | collective-permute-start | bytes 1572872 | tf_op jit(solution)/shard_map/ppermute | solution.py:77
  63.0 27.5 %collective-permute-start.7 = (bf16[256,1024]{1,0:T(8,128)(2,1)S(1)}, bf16[256,1024]{1,0:T(8,128)(2,1)S(1)}, u32[]{:S(2)}, u32[]{:S(2)}) collective-permute-start(bf16[256,1024]{1,0:T(8,128)(2,1)S(1)} %get-tuple-element.28), channel_id=1, source_target_pairs={{0,4},{4,0},{8,12},{12,8},{16,20},{20,16},{24,28},{28,24},{1,5},{5... | collective-permute-start | bytes 1572872 | tf_op jit(solution)/shard_map/ppermute | solution.py:80
  65.6 34.9 %collective-permute-start.5 = (bf16[256,1024]{1,0:T(8,128)(2,1)}, bf16[256,1024]{1,0:T(8,128)(2,1)S(1)}, u32[]{:S(2)}, u32[]{:S(2)}) collective-permute-start(bf16[256,1024]{1,0:T(8,128)(2,1)} %get-tuple-element.27), channel_id=1, source_target_pairs={{0,4},{4,0},{8,12},{12,8},{16,20},{20,16},{24,28},{28,24},{1,5},{5... | collective-permute-start | bytes 1572872 | tf_op jit(solution)/shard_map/ppermute | solution.py:78
  79.3 1.2 copy-start.9
  80.5 20.0 %copy-start.4 = (f32[256,1024]{1,0:T(8,128)S(1)}, f32[256,1024]{1,0:T(8,128)}, u32[]{:S(2)}) copy-start(f32[256,1024]{1,0:T(8,128)} %convolution_add_fusion.2) | copy-start | bytes 3145732
  90.5 0.8 copy-start.13
  105.2 1.5 copy-start.3
  105.3 1.5 copy-start.10
  105.6 1.5 copy-start.7
  162.5 4.6 %copy-start.14 = (f32[3]{0:T(128)}, f32[3]{0:T(128)S(1)}, u32[]{:S(2)}) copy-start(f32[3]{0:T(128)S(1)} %get-tuple-element.24) | copy-start | bytes 40
  163.1 4.1 %copy-start.8 = (f32[256,1024]{1,0:T(8,128)S(1)}, f32[256,1024]{1,0:T(8,128)}, u32[]{:S(2)}) copy-start(f32[256,1024]{1,0:T(8,128)} %fusion.51) | copy-start | bytes 3145732
  163.1 4.1 %copy-start.15 = (f32[256,256]{1,0:T(8,128)S(1)}, f32[256,256]{1,0:T(8,128)}, u32[]{:S(2)}) copy-start(f32[256,256]{1,0:T(8,128)} %get-tuple-element.53) | copy-start | bytes 786436
Sparse Core Ops, SparseCore 0:
  10.7 25.2 all-gather.1

commit v2 on v1

v2 whole, which is shorter than its diff:
```python
import functools

import jax
import jax.numpy as jnp
from jax import lax
from jax.experimental import pallas as pl
from jax.experimental.pallas import tpu as pltpu
from jax.sharding import PartitionSpec as P

EPSILON = 1e-06
CHUNKS = 4
REC = 0
CIRC = 5
MESH = pl.DeviceIdType.MESH
NT = (((1,), (1,)), ((), ()))


def kernel(
    loop_count,
    rep_count,
    circ_ref,
    rec_ref,
    gain_ref,
    scale_ref,
    bias_ref,
    ids_ref,
    out_circ,
    out_rec,
    out_gain,
    out_stat,
    out_loss,
    bufs,
    group,
    inv_circ,
    inv_rec,
    sums,
    red_rep,
    red_dp,
    send_sem,
    recv_sem,
    group_send,
    group_recv,
    rep_send,
    rep_recv,
    dp_send,
    dp_recv,
):
    rows = circ_ref.shape[0]
    step = rows // CHUNKS
    me = lax.axis_index("dp")
    my_rep = lax.axis_index("rep")
    odd = me % 2
    even = 1 - odd
    below = (me + loop_count - 2) % loop_count
    above = (me + 2) % loop_count
    partner = me + 1 - 2 * odd

    barrier = pltpu.get_barrier_semaphore()

    @pl.loop(1, loop_count)
    def _(k):
        pl.semaphore_signal(
            barrier, inc=1, device_id={"dp": (me + k) % loop_count}, device_id_type=MESH
        )

    @pl.loop(1, rep_count)
    def _(k):
        pl.semaphore_signal(
            barrier, inc=1, device_id={"rep": (my_rep + k) % rep_count}, device_id_type=MESH
        )

    def piece(slot, c):
        return bufs.at[slot, pl.ds(c * step, step)]

    def transfer(message, source, target, device, c):
        return pltpu.make_async_remote_copy(
            src_ref=piece(source, c),
            dst_ref=piece(target, c),
            send_sem=send_sem.at[message, c],
            recv_sem=recv_sem.at[target, c],
            device_id={"dp": device},
            device_id_type=MESH,
        )

    rec_two = (0, REC, REC + 2, below)
    circ_two = (1, CIRC, CIRC + 2, above)
    rec_four = (2, REC + 2, REC + 4, below)
    circ_four = (3, CIRC + 2, CIRC + 4, above)
    swap_own = (4, even * CIRC, even * (CIRC + 1) + odd * (REC + 1), partner)
    swap_rec = (5, REC + 2, even * (REC + 1) + odd * (REC + 3), partner)
    swap_circ = (6, CIRC + 2, even * (CIRC + 3) + odd * (CIRC + 1), partner)
    swap_last = (
        7,
        even * (REC + 4) + odd * (CIRC + 4),
        even * (REC + 3) + odd * (CIRC + 3),
        partner,
    )
    messages = (
        rec_two,
        circ_two,
        rec_four,
        circ_four,
        swap_own,
        swap_rec,
        swap_circ,
        swap_last,
    )

    def arrived(slot, c):
        transfer(0, slot, slot, partner, c).wait_recv()

    def group_copy(k):
        return pltpu.make_async_remote_copy(
            src_ref=bufs.at[REC],
            dst_ref=group.at[rep_count - k],
            send_sem=group_send.at[k],
            recv_sem=group_recv.at[rep_count - k],
            device_id={"rep": (my_rep + k) % rep_count},
            device_id_type=MESH,
        )

    multiplier = jnp.exp(jnp.full((1, 1), scale_ref[0], jnp.float32))
    bias_value = bias_ref[0]

    pl.semaphore_wait(barrier, loop_count + rep_count - 2)

    for c in range(CHUNKS):
        part = pl.ds(c * step, step)
        values = rec_ref[part].astype(jnp.float32) * gain_ref[...]
        inverse = lax.rsqrt(jnp.sum(values * values, axis=-1, keepdims=True) + EPSILON)
        inv_rec[part] = inverse
        bufs[REC, part] = (values * inverse).astype(jnp.bfloat16)
        transfer(*rec_two, c).start()
        values = circ_ref[part].astype(jnp.float32)
        inverse = lax.rsqrt(jnp.sum(values * values, axis=-1, keepdims=True) + EPSILON)
        inv_circ[part] = inverse
        bufs[CIRC, part] = (values * inverse).astype(jnp.bfloat16)
        transfer(*circ_two, c).start()
        transfer(*swap_own, c).start()

    @pl.loop(1, rep_count)
    def _(k):
        group_copy(k).start()

    group[0] = bufs[REC]
    sums[...] = jnp.zeros_like(sums)

    def add_sums(weights, scores, losses):
        sums[0:1] += jnp.sum(weights * (scores - bias_value), axis=0, keepdims=True)
        sums[1:2] += jnp.sum(weights, axis=0, keepdims=True)
        sums[2:3] += jnp.sum(losses, axis=0, keepdims=True)

    def score(left, right):
        products = lax.dot_general(left, right, NT, preferred_element_type=jnp.float32)
        return products * multiplier + bias_value

    def sigmoid_and_loss(scores):
        small = jnp.exp(-jnp.abs(scores))
        weights = jnp.where(scores >= 0, 1.0, small) / (1.0 + small)
        return weights, jnp.maximum(scores, 0.0) + jnp.log1p(small)

    def diagonal():
        shape = (rows, rows)
        same = lax.broadcasted_iota(jnp.int32, shape, 0) == lax.broadcasted_iota(
            jnp.int32, shape, 1
        )
        return jnp.where(same, 1.0, 0.0)

    def rec_tile(offset):
        other = bufs[REC + offset]
        scores = score(bufs[CIRC], other)
        weights, losses = sigmoid_and_loss(scores)
        if offset == 0:
            mask = diagonal()
            weights = weights - mask
            losses = losses - scores * mask
        add_sums(weights, scores, losses)
        term = jnp.dot(weights.astype(jnp.bfloat16), other, preferred_element_type=jnp.float32)
        if offset == 0:
            out_circ[...] = term
        else:
            out_circ[...] += term

    def circ_tile(offset):
        other = bufs[CIRC + offset]
        weights, _ = sigmoid_and_loss(score(bufs[REC], other))
        if offset == 0:
            weights = weights - diagonal()
        term = jnp.dot(weights.astype(jnp.bfloat16), other, preferred_element_type=jnp.float32)
        if offset == 0:
            out_rec[...] = term
        else:
            out_rec[...] += term

    def hard_tile(k):
        other = group[k]
        scores = score(bufs[CIRC], other)
        sigmoids, losses = sigmoid_and_loss(scores)
        first = (me * rep_count + (my_rep + k) % rep_count) * rows
        named = lax.broadcasted_iota(jnp.int32, (rows, rows), 1) + first
        times = jnp.zeros((rows, rows), jnp.float32)
        for entry in range(ids_ref.shape[1]):
            times = times + jnp.where(ids_ref[:, entry : entry + 1] == named, 1.0, 0.0)
        add_sums(times * sigmoids, scores, times * losses)
        narrow = times * sigmoids.astype(jnp.bfloat16).astype(jnp.float32)
        out_circ[...] += jnp.dot(
            narrow.astype(jnp.bfloat16), other, preferred_element_type=jnp.float32
        )

    def forward_two(c):
        arrived(REC + 2, c)
        transfer(*rec_four, c).start()
        transfer(*swap_rec, c).start()
        arrived(CIRC + 2, c)
        transfer(*circ_four, c).start()
        transfer(*swap_circ, c).start()

    def forward_four(c):
        arrived(even * (REC + 4) + odd * (CIRC + 4), c)
        transfer(*swap_last, c).start()
        arrived(odd * (REC + 4) + even * (CIRC + 4), c)

    rec_tile(0)
    forward_two(0)
    circ_tile(0)
    forward_two(1)
    hard_tile(0)
    forward_two(2)
    forward_two(3)
    rec_tile(2)
    forward_four(0)
    circ_tile(2)
    forward_four(1)

    @pl.loop(1, rep_count)
    def _(k):
        group_copy(rep_count - k).wait_recv()
        hard_tile(k)

    forward_four(2)
    forward_four(3)
    for c in range(CHUNKS):
        arrived(REC + 1, c)
        arrived(CIRC + 1, c)
    rec_tile(1)
    circ_tile(1)
    rec_tile(4)
    circ_tile(4)
    for c in range(CHUNKS):
        arrived(CIRC + 3, c)
    circ_tile(3)

    gain_part = jnp.zeros((1, rec_ref.shape[1]), jnp.float32)
    for c in range(CHUNKS):
        part = pl.ds(c * step, step)
        values = rec_ref[part].astype(jnp.float32)
        inverse = inv_rec[part]
        unit = values * gain_ref[...] * inverse
        grad = out_rec[part] * multiplier
        along = jnp.sum(unit * grad, axis=-1, keepdims=True)
        grad = (grad - unit * along) * inverse
        gain_part = gain_part + jnp.sum(values * grad, axis=0, keepdims=True)
        out_rec[part] = grad * gain_ref[...]

    for c in range(CHUNKS):
        arrived(REC + 3, c)
    rec_tile(3)

    lane = lax.broadcasted_iota(jnp.int32, (1, rec_ref.shape[1]), 1)
    totals = jnp.sum(sums[...], axis=-1, keepdims=True)
    packed = jnp.zeros((1, rec_ref.shape[1]), jnp.float32)
    for entry in range(3):
        packed = packed + jnp.where(lane == entry, totals[entry : entry + 1], 0.0)
    red_rep[my_rep, 0:1] = gain_part
    red_rep[my_rep, 1:2] = packed

    def rep_copy(k, slot):
        return pltpu.make_async_remote_copy(
            src_ref=red_rep.at[slot],
            dst_ref=red_rep.at[slot],
            send_sem=rep_send.at[k],
            recv_sem=rep_recv.at[k],
            device_id={"rep": (my_rep + k) % rep_count},
            device_id_type=MESH,
        )

    def dp_copy(k, slot):
        return pltpu.make_async_remote_copy(
            src_ref=red_dp.at[slot],
            dst_ref=red_dp.at[slot],
            send_sem=dp_send.at[k],
            recv_sem=dp_recv.at[k],
            device_id={"dp": (me + k) % loop_count},
            device_id_type=MESH,
        )

    @pl.loop(1, rep_count)
    def _(k):
        rep_copy(k, my_rep).start()

    for c in range(CHUNKS):
        part = pl.ds(c * step, step)
        inverse = inv_circ[part]
        unit = circ_ref[part].astype(jnp.float32) * inverse
        grad = out_circ[part] * multiplier
        along = jnp.sum(unit * grad, axis=-1, keepdims=True)
        out_circ[part] = (grad - unit * along) * inverse

    @pl.loop(1, rep_count)
    def _(k):
        rep_copy(k, (my_rep + rep_count - k) % rep_count).wait_recv()

    red_dp[me] = jnp.sum(red_rep[...], axis=0)

    @pl.loop(1, loop_count)
    def _(k):
        dp_copy(k, me).start()

    for message in messages:
        for c in range(CHUNKS):
            transfer(*message, c).wait_send()

    @pl.loop(1, rep_count)
    def _(k):
        group_copy(k).wait_send()
        rep_copy(k, my_rep).wait_send()

    @pl.loop(1, loop_count)
    def _(k):
        dp_copy(k, (me + loop_count - k) % loop_count).wait_recv()

    final = jnp.sum(red_dp[...], axis=0)
    out_gain[...] = final[0:1]
    out_stat[...] = final[1:2, 0:2]
    out_loss[...] = final[1:2, 2:3] * (1.0 / (rows * loop_count * rep_count))

    @pl.loop(1, loop_count)
    def _(k):
        dp_copy(k, me).wait_send()


def per_device(loop_count, rep_count, circuits, records, record_gain, log_scale, logit_bias, ids):
    rows, width = circuits.shape
    vmem = pl.BlockSpec(memory_space=pltpu.VMEM)
    smem = pl.BlockSpec(memory_space=pltpu.SMEM)
    dma = pltpu.SemaphoreType.DMA
    grad_circuits, grad_records, gain, stat, loss = pl.pallas_call(
        functools.partial(kernel, loop_count, rep_count),
        out_shape=(
            jax.ShapeDtypeStruct((rows, width), jnp.float32),
            jax.ShapeDtypeStruct((rows, width), jnp.float32),
            jax.ShapeDtypeStruct((1, width), jnp.float32),
            jax.ShapeDtypeStruct((1, 2), jnp.float32),
            jax.ShapeDtypeStruct((1, 1), jnp.float32),
        ),
        in_specs=[vmem, vmem, vmem, smem, smem, vmem],
        out_specs=(vmem,) * 5,
        scratch_shapes=[
            pltpu.VMEM((10, rows, width), jnp.bfloat16),
            pltpu.VMEM((rep_count, rows, width), jnp.bfloat16),
            pltpu.VMEM((rows, 1), jnp.float32),
            pltpu.VMEM((rows, 1), jnp.float32),
            pltpu.VMEM((3, rows), jnp.float32),
            pltpu.VMEM((rep_count, 2, width), jnp.float32),
            pltpu.VMEM((loop_count, 2, width), jnp.float32),
            dma((8, CHUNKS)),
            dma((10, CHUNKS)),
            dma((rep_count,)),
            dma((rep_count,)),
            dma((rep_count,)),
            dma((rep_count,)),
            dma((loop_count,)),
            dma((loop_count,)),
        ],
        compiler_params=pltpu.CompilerParams(
            collective_id=0, has_side_effects=True, vmem_limit_bytes=48 * 1024 * 1024
        ),
    )(circuits, records, record_gain.reshape(1, width), log_scale, logit_bias, ids)
    return (grad_circuits, grad_records, gain.reshape(width), stat.reshape(2), loss.reshape(1))


def solution(mesh):
    split = P(("dp", "rep"), None)
    return jax.shard_map(
        functools.partial(per_device, mesh.shape["dp"], mesh.shape["rep"]),
        mesh=mesh,
        in_specs=(split, split, P(), P(), P(), split),
        out_specs=(split, split, P(), P(), P()),
        check_vma=False,
    )
```

time: 179 us -> 76 us (0.42)
  Pallas kernels: 0 us -> 66 us
  waiting for transfers between devices: 48.6 us -> 0 us
  blocking collectives: 39.1 us -> 0 us
  matrix products: 36.1 us -> 0 us
  other arithmetic: 20.3 us -> 0 us
  starting transfers between devices: 15.7 us -> 0 us
  between operations: 17.4 us -> 3.69 us
  local copies, waits for them, and re-layouts: 1.44 us -> 5.95 us
    pallas_call x0 -> x1, Pallas kernels: none -> 66 us  [per_device(): pl.pallas_call(functools.partial(kernel, loop_count, rep_count), out_shap...]
    ppermute x8 -> x0, waiting for transfers between devices: 48.6 us -> none  [the longest x4 24.2 us: shifted(): return lax.ppermute(value, axis, pairs)]
    psum x1 -> x0, blocking collectives: 39.1 us -> none  [per_device(): gain_total, summary_total = lax.psum((gain_part, summary), ('dp', 'rep'))]
    dot_general x17 -> x0, matrix products: 36.1 us -> none  [the longest x5 12.3 us: transposed_product(): lax.dot_general(left, right, (((0,), (0,)), ((), ())), preferred_element_...]
    ppermute x8 -> x0, starting transfers between devices: 15.7 us -> none  [the longest x4 11 us: shifted(): return lax.ppermute(value, axis, pairs)]
    add x2 -> x0, other arithmetic: 11.1 us -> none  [the longest x1 11.1 us: per_device(): summary + jnp.stack([jnp.sum(weights * (scores - bias_value)), jnp.sum(we...]
    unnamed x32 -> x11, local copies, waits for them, and re-layouts: 0.84 us -> 5.95 us
    select_n x2 -> x0, other arithmetic: 2.74 us -> none  [the longest x1 1.57 us: per_device(): rec1 = lax.ppermute(jnp.where(even, rec2, rec_emb), 'dp', swap)]
  transfers between devices with their start and end apart: 9 -> 0, of which waited for: 7 -> 0; matrix products, arithmetic and copies ran while one was open for 17% -> 0% of each run, Pallas kernels for 0% -> 0%
where the time goes in v2:
time: 76 us; the launch traced here: 75.7 us
  Pallas kernels  66 us (87%)
  local copies, waits for them, and re-layouts  5.95 us (8%)
  between operations  3.69 us (5%)
    pallas_call x1, Pallas kernels, per_device(): pl.pallas_call(functools.partial(kernel, loop_count, rep_count), out_shap...  66 us
    unnamed x11, local copies, waits for them, and re-layouts  5.95 us

profile of v2, /device:TPU:0, one launch (start us, length us, event | category | flops | bytes accessed | tf_op | source)
XLA Modules:
  0.0 75.7 jit_solution(9820074843016338546)
XLA Ops:
  1.9 0.0 copy-start.2
  1.9 0.8 %copy.11.ids_ref = s32[256,16]{1,0:T(8,128)S(1)} copy(s32[256,16]{0,1:T(8,128)} %param.11) | data formatting | bytes 32768 | tf_op args[5]
  2.8 0.0 copy-done.2
  2.8 0.0 copy-start
  2.8 1.0 %copy-done = bf16[256,1024]{1,0:T(8,128)(2,1)S(1)} copy-done((bf16[256,1024]{1,0:T(8,128)(2,1)S(1)}, bf16[256,1024]{1,0:T(8,128)(2,1)}, u32[]{:S(2)}) %copy-start) | copy-done | bytes 524312
  3.8 0.0 copy-start.1
  3.8 1.0 %copy-done.1 = bf16[256,1024]{1,0:T(8,128)(2,1)S(1)} copy-done((bf16[256,1024]{1,0:T(8,128)(2,1)S(1)}, bf16[256,1024]{1,0:T(8,128)(2,1)}, u32[]{:S(2)}) %copy-start.1) | copy-done | bytes 524312
  4.8 66.0 %shard_map.101 = (f32[256,1024]{1,0:T(8,128)S(1)}, f32[256,1024]{1,0:T(8,128)S(1)}, f32[1,1024]{1,0:T(1,128)S(1)}, f32[1,2]{1,0:T(1,128)S(1)}, f32[1,1]{1,0:T(1,128)}) custom-call(bf16[256,1024]{1,0:T(8,128)(2,1)S(1)} %copy-done, bf16[256,1024]{1,0:T(8,128)(2,1)S(1)} %copy-done.1, f32[1,1024]{1,0:T(1,128)S(1)} %bitcast.4, f32[1]{0:T(128)S(6)} %copy.17.scale_ref, ...), custom_call_target="tpu_custom_call" | custom-call | tf_op jit(solution)/shard_map/pallas_call | solution.py:347
  70.9 1.0 %copy.19 = f32[256,1024]{1,0:T(8,128)} copy(f32[256,1024]{1,0:T(8,128)S(1)} %get-tuple-element.20) | data formatting | bytes 2097152
  71.9 1.0 %copy.20 = f32[256,1024]{1,0:T(8,128)} copy(f32[256,1024]{1,0:T(8,128)S(1)} %get-tuple-element.21) | data formatting | bytes 2097152
  72.8 0.6 copy.21
  73.4 0.5 copy.22
Async XLA Ops:
  1.9 0.8 %copy-start.2 = (f32[1024]{0:T(1024)S(1)}, f32[1024]{0:T(1024)}, u32[]{:S(2)}) copy-start(f32[1024]{0:T(1024)} %param.8) | copy-start | bytes 12292
  2.8 1.0 %copy-start = (bf16[256,1024]{1,0:T(8,128)(2,1)S(1)}, bf16[256,1024]{1,0:T(8,128)(2,1)}, u32[]{:S(2)}) copy-start(bf16[256,1024]{1,0:T(8,128)(2,1)} %circ_ref.1) | copy-start | bytes 1572868
  3.8 1.0 %copy-start.1 = (bf16[256,1024]{1,0:T(8,128)(2,1)S(1)}, bf16[256,1024]{1,0:T(8,128)(2,1)}, u32[]{:S(2)}) copy-start(bf16[256,1024]{1,0:T(8,128)(2,1)} %rec_ref.1) | copy-start | bytes 1572868
